TPU v7x, 256 devices: a whole 4x4x8 slice. The times are simulated.
256 devices in a mesh: gx: 32 (over x, z), gy: 8 (over y, core).
Axes of the slice: x: 4, y: 4, z: 8, core: 2. Of those that a mesh axis runs over, the one named last changes fastest.
Arguments:
- depth: float32 [4096, 4096], P('gx', 'gy'), may hold values from 0.3 to 1.2
- momentum_x: float32 [4096, 4096], P('gx', 'gy'), may hold values from -3 to 3
- momentum_y: float32 [4096, 4096], P('gx', 'gy'), may hold values from -3 to 3
- bed: float32 [4096, 4096], P('gx', 'gy'), may hold values from -1 to 1
- wet: int32 [4096, 4096], P('gx', 'gy'), may hold values 0 or 1
Outputs:
- new_depth: float32 [4096, 4096], P('gx', 'gy')
- velocity_x: float32 [4096, 4096], P('gx', 'gy')
- velocity_y: float32 [4096, 4096], P('gx', 'gy')
All inputs are finite; a program needn't handle non-finite values. No bound on the sum of `wet` on one device may be relied on, other than what follows from the above.
Results may differ from a plain program's by a relative error of at most 0.0013.
Values sent between devices are 32-bit elements; how exact they have to be, the bound alone decides.
A program may use at most 64 MiB of HBM per device.

v0:
```python
import jax
import jax.numpy as jnp
from jax import lax
from jax.sharding import PartitionSpec as P

gravity = 9.81
ratio_x = 0.05
ratio_y = 0.05


def with_halo(block, sides, width):
    for axis, dim in sides:
        count = lax.axis_size(axis)
        forward = [(i, i + 1) for i in range(count - 1)]
        backward = [(target, source) for source, target in forward]
        low = lax.ppermute(
            lax.slice_in_dim(block, block.shape[dim] - width, None, axis=dim), axis, forward
        )
        high = lax.ppermute(lax.slice_in_dim(block, 0, width, axis=dim), axis, backward)
        block = jnp.concatenate([low, block, high], axis=dim)
    return block


def minmod(left, right):
    return 0.5 * (jnp.sign(left) + jnp.sign(right)) * jnp.minimum(jnp.abs(left), jnp.abs(right))


def window(values, start, stop, line_axis):
    return lax.slice_in_dim(values, start, stop, axis=line_axis)


def physical(height, normal, across):
    speed_n = normal / height
    fluxes = (normal, normal * speed_n + 0.5 * gravity * height * height, across * speed_n)
    return (fluxes, jnp.abs(speed_n) + jnp.sqrt(gravity * height))


def face_terms(depth, normal, across, wet_cells, line_axis):
    length = depth.shape[line_axis]
    states = (depth, normal, across)
    slopes = [
        minmod(
            window(field, 1, length - 1, line_axis) - window(field, 0, length - 2, line_axis),
            window(field, 2, length, line_axis) - window(field, 1, length - 1, line_axis),
        )
        for field in states
    ]
    lefts = [
        window(field, 1, length - 2, line_axis) + 0.5 * window(slope, 0, length - 3, line_axis)
        for field, slope in zip(states, slopes)
    ]
    rights = [
        window(field, 2, length - 1, line_axis) - 0.5 * window(slope, 1, length - 2, line_axis)
        for field, slope in zip(states, slopes)
    ]
    opened = window(wet_cells, 1, length - 2, line_axis) * window(
        wet_cells, 2, length - 1, line_axis
    )
    safe_left = jnp.where(opened > 0.5, lefts[0], 1.0)
    safe_right = jnp.where(opened > 0.5, rights[0], 1.0)
    flux_left, speed_left = physical(safe_left, lefts[1], lefts[2])
    flux_right, speed_right = physical(safe_right, rights[1], rights[2])
    fastest = jnp.maximum(speed_left, speed_right)
    result = []
    for flux_a, flux_b, state_a, state_b in zip(flux_left, flux_right, lefts, rights):
        face = opened * (0.5 * (flux_a + flux_b) - 0.5 * fastest * (state_b - state_a))
        count = face.shape[line_axis]
        result.append(window(face, 1, count, line_axis) - window(face, 0, count - 1, line_axis))
    return result


def predict(padded):
    along_x = padded[:, :, 2:-2]
    along_y = padded[:, 2:-2, :]
    center = padded[:, 2:-2, 2:-2]
    depth, flow_x, flow_y, wet_cells = (center[0], center[1], center[2], center[4])
    mass_x, normal_x, shear_x = face_terms(along_x[0], along_x[1], along_x[2], along_x[4], 0)
    mass_y, normal_y, shear_y = face_terms(along_y[0], along_y[2], along_y[1], along_y[4], 1)
    bed_x = 0.5 * (along_x[3, 3:-1] - along_x[3, 1:-3])
    bed_y = 0.5 * (along_y[3, :, 3:-1] - along_y[3, :, 1:-3])
    new_depth = depth - wet_cells * (ratio_x * mass_x + ratio_y * mass_y)
    push_x = wet_cells * (
        flow_x - ratio_x * normal_x - ratio_y * shear_y - ratio_x * gravity * depth * bed_x
    )
    push_y = wet_cells * (
        flow_y - ratio_x * shear_x - ratio_y * normal_y - ratio_y * gravity * depth * bed_y
    )
    return (new_depth, push_x, push_y)


def earlier(values, stride, line_axis, fill):
    which = line_axis % values.ndim
    widths = [(0, 0)] * values.ndim
    widths[which] = (stride, 0)
    padded = jnp.pad(values, widths, constant_values=fill)
    return lax.slice_in_dim(padded, 0, values.shape[which], axis=which)


def later(values, stride, line_axis, fill):
    which = line_axis % values.ndim
    widths = [(0, 0)] * values.ndim
    widths[which] = (0, stride)
    padded = jnp.pad(values, widths, constant_values=fill)
    return lax.slice_in_dim(padded, stride, stride + values.shape[which], axis=which)


def eliminate(rows, below, above):
    lower, diagonal, upper, right = rows
    left_factor = lower / below[1]
    right_factor = upper / above[1]
    return (
        -left_factor * below[0],
        diagonal - left_factor * below[2] - right_factor * above[0],
        -right_factor * above[2],
        right - left_factor * below[3] - right_factor * above[3],
    )


def reduce_lines(lower, diagonal, upper, right, line_axis):
    count = diagonal.shape[line_axis % diagonal.ndim]
    rows = (lower, diagonal, upper, right)
    stride = 1
    while stride < count:
        below = tuple(
            (
                earlier(member, stride, line_axis, fill)
                for member, fill in zip(rows, (0.0, 1.0, 0.0, 0.0))
            )
        )
        above = tuple(
            (
                later(member, stride, line_axis, fill)
                for member, fill in zip(rows, (0.0, 1.0, 0.0, 0.0))
            )
        )
        rows = lax.optimization_barrier(eliminate(rows, below, above))
        stride *= 2
    return rows[3] / rows[1]


def separator_rows(last_six, next_three):
    solved_y, solved_g, solved_e, sep_coef, sep_diag, sep_right = last_six
    first_y, first_g, first_e = next_three
    return (
        -sep_coef * solved_g,
        sep_diag - sep_coef * solved_e - sep_coef * first_g,
        -sep_coef * first_e,
        sep_right + sep_coef * solved_y + sep_coef * first_y,
    )


def local_spikes(coefficient, right, line_axis):
    which = line_axis % 2
    count = coefficient.shape[which]
    inner = lax.slice_in_dim(coefficient, 0, count - 1, axis=which)
    position = lax.broadcasted_iota(jnp.int32, inner.shape, which)
    zeros = jnp.zeros_like(inner)
    sources = jnp.stack(
        [
            lax.slice_in_dim(right, 0, count - 1, axis=which),
            jnp.where(position == 0, inner, zeros),
            jnp.where(position == count - 2, inner, zeros),
        ]
    )
    solved = reduce_lines(-inner, 1.0 + 2.0 * inner, -inner, sources, line_axis)
    first = lax.index_in_dim(solved, 0, which + 1, keepdims=False)
    final = lax.index_in_dim(solved, count - 2, which + 1, keepdims=False)
    sep_coef = lax.index_in_dim(coefficient, count - 1, which, keepdims=False)
    sep_right = lax.index_in_dim(right, count - 1, which, keepdims=False)
    last_six = jnp.concatenate([final, jnp.stack([sep_coef, 1.0 + 2.0 * sep_coef, sep_right])])
    return (solved, first, last_six)


def assemble(solved, own, previous, line_axis):
    which = line_axis % 2
    own_wide = jnp.expand_dims(own, which)
    prev_wide = jnp.expand_dims(previous, which)
    inner = solved[0] + solved[1] * prev_wide + solved[2] * own_wide
    return jnp.concatenate([inner, own_wide], axis=which)


def pick_rows(whole, index):
    first_all = whole[:3]
    rows = separator_rows(whole[3:], later(first_all, 1, -2, 0.0))
    solved = reduce_lines(rows[0], rows[1], rows[2], rows[3], -2)
    own = lax.dynamic_index_in_dim(solved, index, 0, keepdims=False)
    previous = lax.dynamic_index_in_dim(earlier(solved, 1, -2, 0.0), index, 0, keepdims=False)
    return (own, previous)


def interface_x(first, last_six):
    packed = jnp.concatenate([first, last_six])[:, None, :]
    whole = lax.all_gather(packed, "gx", axis=1, tiled=True)
    return pick_rows(whole, lax.axis_index("gx"))


def interface_y(first, last_six):
    packed = jnp.concatenate([first, last_six])[:, None, :]
    whole = lax.all_gather(packed, "gy", axis=1, tiled=True)
    return pick_rows(whole, lax.axis_index("gy"))


def on_device(depth, momentum_x, momentum_y, bed, wet):
    stacked = jnp.stack([depth, momentum_x, momentum_y, bed, wet.astype(jnp.float32)])
    padded = with_halo(stacked, (("gx", 1), ("gy", 2)), 2)
    new_depth, push_x, push_y = predict(padded)
    cells_x = depth.shape[0] * lax.axis_size("gx")
    cells_y = depth.shape[1] * lax.axis_size("gy")
    scale_x = (cells_x / 4.0) ** 2 / 3.0
    scale_y = (cells_y / 4.0) ** 2 / 3.0
    coef_x = scale_x * depth * depth
    coef_y = scale_y * depth * depth
    solved_x, first_x, last_x = local_spikes(coef_x, push_x, -2)
    own_x, prev_x = interface_x(first_x, last_x)
    flux_u = assemble(solved_x, own_x, prev_x, -2)
    solved_y, first_y, last_y = local_spikes(coef_y, push_y, -1)
    own_y, prev_y = interface_y(first_y, last_y)
    flux_v = assemble(solved_y, own_y, prev_y, -1)
    return (new_depth, flux_u / depth, flux_v / depth)


def solution(mesh):
    placed = (P("gx", "gy"), P("gx", "gy"), P("gx", "gy"), P("gx", "gy"), P("gx", "gy"))
    return jax.shard_map(
        on_device,
        mesh=mesh,
        in_specs=placed,
        out_specs=(P("gx", "gy"), P("gx", "gy"), P("gx", "gy")),
        check_vma=False,
    )
```

profile of v0, /device:TPU:8, one launch (start us, length us, event | category | flops | bytes accessed | tf_op | source)
XLA Modules:
  0.0 121.2 jit_solution(9153613067700028402)
XLA Ops:
  0.7 1.0 bitcast_dynamic-update-slice_fusion.4
  1.7 1.0 bitcast_dynamic-update-slice_fusion.3
  2.7 1.0 bitcast_dynamic-update-slice_fusion.2
  3.7 3.8 %collective-permute-start = (f32[5,2,512]{2,1,0:T(2,128)S(1)}, f32[5,2,512]{2,1,0:T(2,128)S(1)}, u32[]{:S(2)}, u32[]{:S(2)}) collective-permute-start(f32[5,2,512]{2,1,0:T(2,128)S(1)} %get-tuple-element.274), channel_id=1, source_target_pairs={{0,8},{8,16},{16,24},{24,32},{32,40},{40,48},{48,56},{56,64},{64,7... | collective-permute-start | bytes 61448 | tf_op jit(solution)/shard_map/ppermute | solution.py:16
  7.6 1.3 %collective-permute-start.1 = (f32[5,2,512]{2,1,0:T(2,128)S(1)}, f32[5,2,512]{2,1,0:T(2,128)S(1)}, u32[]{:S(2)}, u32[]{:S(2)}) collective-permute-start(f32[5,2,512]{2,1,0:T(2,128)S(1)} %get-tuple-element.275), channel_id=1, source_target_pairs={{8,0},{16,8},{24,16},{32,24},{40,32},{48,40},{56,48},{64,56},{72,6... | collective-permute-start | bytes 61448 | tf_op jit(solution)/shard_map/ppermute | solution.py:19
  9.5 3.8 %collective-permute-done.1 = f32[5,2,512]{2,1,0:T(2,128)S(1)} collective-permute-done((f32[5,2,512]{2,1,0:T(2,128)S(1)}, f32[5,2,512]{2,1,0:T(2,128)S(1)}, u32[]{:S(2)}, u32[]{:S(2)}) %collective-permute-start.1) | collective-permute-done | bytes 20512 | tf_op jit(solution)/shard_map/ppermute | solution.py:19
  13.7 1.9 %collective-permute-start.2 = (f32[5,132,2]{2,1,0:T(8,128)S(1)}, f32[5,132,2]{2,1,0:T(8,128)S(1)}, u32[]{:S(2)}, u32[]{:S(2)}) collective-permute-start(f32[5,132,2]{2,1,0:T(8,128)S(1)} %get-tuple-element.272), channel_id=1, source_target_pairs={{0,1},{1,2},{2,3},{3,4},{4,5},{5,6},{6,7},{8,9},{9,10},{10,11},{11... | collective-permute-start | bytes 15848 | tf_op jit(solution)/shard_map/ppermute | solution.py:16
  15.6 3.6 %collective-permute-start.3 = (f32[5,132,2]{2,1,0:T(8,128)S(1)}, f32[5,132,2]{2,1,0:T(8,128)S(1)}, u32[]{:S(2)}, u32[]{:S(2)}) collective-permute-start(f32[5,132,2]{2,1,0:T(8,128)S(1)} %get-tuple-element.273), channel_id=1, source_target_pairs={{1,0},{2,1},{3,2},{4,3},{5,4},{6,5},{7,6},{9,8},{10,9},{11,10},{12... | collective-permute-start | bytes 15848 | tf_op jit(solution)/shard_map/ppermute | solution.py:19
  19.3 1.5 %minimum_multiply_fusion.4 = (f32[1,130,512]{2,1,0:T(8,128)S(1)}, f32[1,130,512]{2,1,0:T(8,128)S(1)}, f32[1,130,512]{2,1,0:T(8,128)S(1)}) fusion(f32[5,2,512]{2,1,0:T(2,128)} %copy-done.15, f32[5,128,512]{2,1,0:T(8,128)S(1)} %bitcast_dynamic-update-slice_fusion, f32[5,2,512]{2,1,0:T(2,128)} %copy-done.12, f32[5,132,512]{2,1,0:T(8,128)S(1)} %pad_maximum_fusion), kind=kLoop, calls=%fused_computation.293 | loop fusion | flops 2396160 | bytes 2949120 | tf_op jit(solution)/shard_map/mul | solution.py:25
  21.4 1.2 fusion.73
  22.5 1.5 %collective-permute-done.3 = f32[5,132,2]{2,1,0:T(8,128)S(1)} collective-permute-done((f32[5,132,2]{2,1,0:T(8,128)S(1)}, f32[5,132,2]{2,1,0:T(8,128)S(1)}, u32[]{:S(2)}, u32[]{:S(2)}) %collective-permute-start.3) | collective-permute-done | bytes 5312 | tf_op jit(solution)/shard_map/ppermute | solution.py:19
  24.8 1.3 %minimum_multiply_fusion = (f32[128,514]{1,0:T(8,128)}, f32[128,514]{1,0:T(8,128)S(1)}) fusion(f32[128,516]{1,0:T(8,128)S(1)} %get-tuple-element.267, f32[128,516]{1,0:T(8,128)S(1)} %get-tuple-element.268), kind=kLoop, calls=%fused_computation.214 | loop fusion | flops 1315840 | bytes 2105344 | tf_op jit(solution)/shard_map/mul | solution.py:25
  26.2 0.8 subtract_multiply_fusion.1
  27.0 0.8 fusion.60
  28.1 1.1 fusion.232
  39.0 0.9 copy-done
  40.7 1.3 %concatenate.52 = f32[9,128]{1,0:T(8,128)S(1)} concatenate(f32[3,128]{1,0:T(4,128)S(1)} %get-tuple-element.189, f32[3,128]{1,0:T(4,128)S(1)} %get-tuple-element.188, f32[1,128]{1,0:T(1,128)} %bitcast.173, f32[1,128]{1,0:T(1,128)} %multiply_add_fusion.3, f32[1,128]{1,0:T(1,128)} %bitcast.174), dimensions={0} | concatenate | bytes 9216 | tf_op jit(solution)/shard_map/concatenate | solution.py:198
  42.0 13.1 %all-gather.1 = f32[9,1024]{1,0:T(8,128)S(1)} all-gather(f32[9,128]{1,0:T(8,128)S(1)} %concatenate.52), channel_id=3, replica_groups=mesh['gx'=32,'gy'=8] {'gy'}, dimensions={1}, use_global_device_ids=true | all-gather | bytes 41472 | tf_op jit(solution)/shard_map/all_gather | solution.py:199
  55.1 0.9 multiply_add_fusion.1
  56.0 1.8 %subtract_multiply_fusion = f32[128,513]{1,0:T(8,128)} fusion(f32[128,514]{1,0:T(8,128)S(1)} %copy-done.4, f32[128,516]{1,0:T(8,128)S(1)} %get-tuple-element.267, f32[128,516]{1,0:T(8,128)S(1)} %maximum_bitcast_fusion.2, f32[128,514]{1,0:T(8,128)S(1)} %minimum_multiply_fusion.2, f32[128,516]{1,0:T(8,128)S(1)} %get-tuple-element.269, ...), kind=kLoop, calls=%fused_computation.213 | loop fusion | flops 2232576 | bytes 3939840 | tf_op jit(solution)/shard_map/mul | solution.py:66
  58.7 1.2 fusion.224
  60.0 2.0 %maximum_divide_fusion.1 = (f32[128,512]{1,0:T(8,128)}, f32[128,512]{1,0:T(8,128)S(1)}) fusion(f32[128,512]{1,0:T(8,128)S(1)} %copy-done.3, f32[128,1]{1,0:T(8,128)} %copy.28, f32[128,511]{1,0:T(8,128)S(1)} %fusion.224, f32[5,128,512]{2,1,0:T(8,128)S(1)} %bitcast_dynamic-update-slice_fusion, f32[5,2,512]{2,1,0:T(2,128)S(1)} %copy-done.14, ...), kind=kLoop, calls=%fused_computation.461 | loop fusion | flops 1114112 | bytes 3973120 | tf_op jit(solution)/shard_map/div | solution.py:219
  65.2 53.4 %all-gather = f32[9,16384]{1,0:T(8,128)S(1)} all-gather(f32[9,512]{1,0:T(8,128)S(1)} %concatenate.48), channel_id=2, replica_groups=mesh['gx'=32,'gy'=8] {'gx'}, dimensions={1}, use_global_device_ids=true | all-gather | bytes 608256 | tf_op jit(solution)/shard_map/all_gather | solution.py:193
  118.6 1.0 slice_reduce_fusion.4
  (167 shorter events, 18.5 us)
Async XLA Ops:
  0.6 3.0 %copy-start.18 = (f32[128,512]{1,0:T(8,128)S(1)}, f32[128,512]{1,0:T(8,128)}, u32[]{:S(2)}) copy-start(f32[128,512]{1,0:T(8,128)} %param.8) | copy-start | bytes 786436
  0.6 3.0 %copy-start.6 = (s32[128,512]{1,0:T(8,128)S(1)}, s32[128,512]{1,0:T(8,128)}, u32[]{:S(2)}) copy-start(s32[128,512]{1,0:T(8,128)} %param.9) | copy-start | bytes 786436
  3.7 5.7 %collective-permute-start = (f32[5,2,512]{2,1,0:T(2,128)S(1)}, f32[5,2,512]{2,1,0:T(2,128)S(1)}, u32[]{:S(2)}, u32[]{:S(2)}) collective-permute-start(f32[5,2,512]{2,1,0:T(2,128)S(1)} %get-tuple-element.274), channel_id=1, source_target_pairs={{0,8},{8,16},{16,24},{24,32},{32,40},{40,48},{48,56},{56,64},{64,7... | collective-permute-start | bytes 61448 | tf_op jit(solution)/shard_map/ppermute | solution.py:16
  7.6 5.7 %collective-permute-start.1 = (f32[5,2,512]{2,1,0:T(2,128)S(1)}, f32[5,2,512]{2,1,0:T(2,128)S(1)}, u32[]{:S(2)}, u32[]{:S(2)}) collective-permute-start(f32[5,2,512]{2,1,0:T(2,128)S(1)} %get-tuple-element.275), channel_id=1, source_target_pairs={{8,0},{16,8},{24,16},{32,24},{40,32},{48,40},{56,48},{64,56},{72,6... | collective-permute-start | bytes 61448 | tf_op jit(solution)/shard_map/ppermute | solution.py:19
  9.5 6.1 %copy-start.12 = (f32[5,2,512]{2,1,0:T(2,128)}, f32[5,2,512]{2,1,0:T(2,128)S(1)}, u32[]{:S(2)}) copy-start(f32[5,2,512]{2,1,0:T(2,128)S(1)} %collective-permute-done) | copy-start | bytes 61444
  13.2 2.4 %copy-start.15 = (f32[5,2,512]{2,1,0:T(2,128)}, f32[5,2,512]{2,1,0:T(2,128)S(1)}, u32[]{:S(2)}) copy-start(f32[5,2,512]{2,1,0:T(2,128)S(1)} %collective-permute-done.1) | copy-start | bytes 61444
  13.7 8.9 %collective-permute-start.2 = (f32[5,132,2]{2,1,0:T(8,128)S(1)}, f32[5,132,2]{2,1,0:T(8,128)S(1)}, u32[]{:S(2)}, u32[]{:S(2)}) collective-permute-start(f32[5,132,2]{2,1,0:T(8,128)S(1)} %get-tuple-element.272), channel_id=1, source_target_pairs={{0,1},{1,2},{2,3},{3,4},{4,5},{5,6},{6,7},{8,9},{9,10},{10,11},{11... | collective-permute-start | bytes 15848 | tf_op jit(solution)/shard_map/ppermute | solution.py:16
  15.6 8.4 %collective-permute-start.3 = (f32[5,132,2]{2,1,0:T(8,128)S(1)}, f32[5,132,2]{2,1,0:T(8,128)S(1)}, u32[]{:S(2)}, u32[]{:S(2)}) collective-permute-start(f32[5,132,2]{2,1,0:T(8,128)S(1)} %get-tuple-element.273), channel_id=1, source_target_pairs={{1,0},{2,1},{3,2},{4,3},{5,4},{6,5},{7,6},{9,8},{10,9},{11,10},{12... | collective-permute-start | bytes 15848 | tf_op jit(solution)/shard_map/ppermute | solution.py:19
  19.3 1.5 %copy-start.13 = (f32[5,2,512]{2,1,0:T(2,128)S(1)}, f32[5,2,512]{2,1,0:T(2,128)}, u32[]{:S(2)}) copy-start(f32[5,2,512]{2,1,0:T(2,128)} %copy-done.12) | copy-start | bytes 61444
  19.3 1.5 %copy-start.16 = (f32[5,2,512]{2,1,0:T(2,128)S(1)}, f32[5,2,512]{2,1,0:T(2,128)}, u32[]{:S(2)}) copy-start(f32[5,2,512]{2,1,0:T(2,128)} %copy-done.15) | copy-start | bytes 61444
  27.0 1.0 copy-start.7
  27.0 1.1 copy-start.11
  29.4 10.8 %copy-start.19 = (f32[128]{0:T(128)}, f32[128]{0:T(128)S(1)}, u32[]{:S(2)}) copy-start(f32[128]{0:T(128)S(1)} %slice_reduce_fusion.3) | copy-start | bytes 1540
  42.0 14.0 %copy-start.4 = (f32[128,514]{1,0:T(8,128)S(1)}, f32[128,514]{1,0:T(8,128)}, u32[]{:S(2)}) copy-start(f32[128,514]{1,0:T(8,128)} %get-tuple-element.331) | copy-start | bytes 789508
  57.8 2.1 %copy-start.3 = (f32[128,512]{1,0:T(8,128)S(1)}, f32[128,512]{1,0:T(8,128)}, u32[]{:S(2)}) copy-start(f32[128,512]{1,0:T(8,128)} %param.5) | copy-start | bytes 786436
  57.8 2.2 %copy-start.8 = (s32[128,512]{1,0:T(8,128)S(1)}, s32[128,512]{1,0:T(8,128)}, u32[]{:S(2)}) copy-start(s32[128,512]{1,0:T(8,128)} %param.9) | copy-start | bytes 786436
  57.8 2.2 %copy-start.9 = (f32[129,512]{1,0:T(8,128)S(1)}, f32[129,512]{1,0:T(8,128)}, u32[]{:S(2)}) copy-start(f32[129,512]{1,0:T(8,128)} %get-tuple-element.270) | copy-start | bytes 792580
  57.8 2.2 %copy-start.10 = (f32[128,513]{1,0:T(8,128)S(1)}, f32[128,513]{1,0:T(8,128)}, u32[]{:S(2)}) copy-start(f32[128,513]{1,0:T(8,128)} %subtract_multiply_fusion) | copy-start | bytes 787972
  57.8 2.2 %copy-start.14 = (f32[5,2,512]{2,1,0:T(2,128)S(1)}, f32[5,2,512]{2,1,0:T(2,128)}, u32[]{:S(2)}) copy-start(f32[5,2,512]{2,1,0:T(2,128)} %copy-done.12) | copy-start | bytes 61444
  57.8 2.2 %copy-start.17 = (f32[5,2,512]{2,1,0:T(2,128)S(1)}, f32[5,2,512]{2,1,0:T(2,128)}, u32[]{:S(2)}) copy-start(f32[5,2,512]{2,1,0:T(2,128)} %copy-done.15) | copy-start | bytes 61444
  60.0 2.1 %copy-start.1 = (f32[127,512]{1,0:T(8,128)S(1)}, f32[127,512]{1,0:T(8,128)}, u32[]{:S(2)}) copy-start(f32[127,512]{1,0:T(8,128)} %get-tuple-element.294) | copy-start | bytes 780292
  60.0 2.1 %copy-start.5 = (f32[127,512]{1,0:T(8,128)S(1)}, f32[127,512]{1,0:T(8,128)}, u32[]{:S(2)}) copy-start(f32[127,512]{1,0:T(8,128)} %get-tuple-element.293) | copy-start | bytes 780292
  60.0 2.1 %copy-start.20 = (pred[127]{0:T(512)(128)(4,1)S(1)}, pred[127]{0:T(512)(128)(4,1)}, u32[]{:S(2)}) copy-start(pred[127]{0:T(512)(128)(4,1)} %get-tuple-element.333) | copy-start | bytes 385
  60.0 2.1 %copy-start.21 = (pred[127]{0:T(512)(128)(4,1)S(1)}, pred[127]{0:T(512)(128)(4,1)}, u32[]{:S(2)}) copy-start(pred[127]{0:T(512)(128)(4,1)} %get-tuple-element.334) | copy-start | bytes 385
  (2 other events, 1.9 us)
where the time goes:
time: 122 us; the launch traced here: 121 us
  blocking collectives  66.5 us (55%)
  other arithmetic  28 us (23%)
  starting transfers between devices  10.7 us (9%)
  local copies, waits for them, and re-layouts  9.07 us (7%)
  waiting for transfers between devices  5.26 us (4%)
  between operations  1.77 us (1%)
    all_gather x1, blocking collectives, interface_x(): whole = lax.all_gather(packed, 'gx', axis=1, tiled=True)  53.4 us
    all_gather x1, blocking collectives, interface_y(): whole = lax.all_gather(packed, 'gy', axis=1, tiled=True)  13.1 us
    ppermute x2, starting transfers between devices, with_halo(): lax.ppermute(lax.slice_in_dim(block, block.shape[dim] - width, None, axis...  5.74 us
    ppermute x2, waiting for transfers between devices, with_halo(): lax.ppermute(lax.slice_in_dim(block, 0, width, axis=dim), axis, backward)  5.26 us
    sub x24, other arithmetic, eliminate(): right - left_factor * below[3] - right_factor * above[3]  5.16 us
    mul x5, other arithmetic, face_terms(): opened * (0.5 * (flux_a + flux_b) - 0.5 * fastest * (state_b - state_a))  5.04 us
    ppermute x2, starting transfers between devices, with_halo(): lax.ppermute(lax.slice_in_dim(block, 0, width, axis=dim), axis, backward)  4.93 us
    unnamed x53, local copies, waits for them, and re-layouts  4.38 us
  transfers between devices with their start and end apart: 4, of which 2 were waited for; matrix products, arithmetic and copies ran while one was open for 3% of the time, Pallas kernels for 0%

commit v1 on v0

--- a/solution.py
+++ b/solution.py
@@ -196,7 +196,8 @@
 
 def interface_y(first, last_six):
     packed = jnp.concatenate([first, last_six])[:, None, :]
-    whole = lax.all_gather(packed, "gy", axis=1, tiled=True)
+    outgoing = jnp.stack([packed] * lax.axis_size("gy"))
+    whole = jnp.concatenate(lax.all_to_all(outgoing, "gy", 0, 0), axis=1)
     return pick_rows(whole, lax.axis_index("gy"))
 
 

time: 122 us -> 115 us (0.943)
  blocking collectives: 66.5 us -> 53.4 us
  starting transfers between devices: 10.7 us -> 16.8 us
  waiting for transfers between devices: 5.26 us -> 8.22 us
  other arithmetic: 28 us -> 25.4 us
    all_gather x1 -> x0, blocking collectives: 13.1 us -> none  [interface_y(): whole = lax.all_gather(packed, 'gy', axis=1, tiled=True)]
    all_to_all x0 -> x1, starting transfers between devices: none -> 6.08 us  [interface_y(): whole = jnp.concatenate(lax.all_to_all(outgoing, 'gy', 0, 0), axis=1)]
    all_to_all x0 -> x1, waiting for transfers between devices: none -> 1.56 us  [interface_y(): whole = jnp.concatenate(lax.all_to_all(outgoing, 'gy', 0, 0), axis=1)]
    mul x3, other arithmetic: 3.05 us -> 1.59 us  [minmod(): 0.5 * (jnp.sign(left) + jnp.sign(right))]
    concatenate x1, local copies, waits for them, and re-layouts: 1.31 us -> 0.04 us  [interface_y(): packed = jnp.concatenate([first, last_six])[:, None, :]]
    unnamed x53 -> x30, local copies, waits for them, and re-layouts: 4.38 us -> 5.64 us
  transfers between devices with their start and end apart: 4 -> 5, of which waited for: 2 -> 5; matrix products, arithmetic and copies ran while one was open for 3% -> 4% of each run, Pallas kernels for 0% -> 0%
where the time goes in v1:
time: 115 us; the launch traced here: 114 us
  blocking collectives  53.4 us (46%)
  other arithmetic  25.4 us (22%)
  starting transfers between devices  16.8 us (15%)
  local copies, waits for them, and re-layouts  8.53 us (7%)
  waiting for transfers between devices  8.22 us (7%)
  between operations  1.62 us (1%)
    all_gather x1, blocking collectives, interface_x(): whole = lax.all_gather(packed, 'gx', axis=1, tiled=True)  53.4 us
    all_to_all x1, starting transfers between devices, interface_y(): whole = jnp.concatenate(lax.all_to_all(outgoing, 'gy', 0, 0), axis=1)  6.08 us
    ppermute x2, waiting for transfers between devices, with_halo(): lax.ppermute(lax.slice_in_dim(block, 0, width, axis=dim), axis, backward)  5.97 us
    ppermute x2, starting transfers between devices, with_halo(): lax.ppermute(lax.slice_in_dim(block, block.shape[dim] - width, None, axis...  5.74 us
    unnamed x30, local copies, waits for them, and re-layouts  5.64 us
    sub x24, other arithmetic, eliminate(): right - left_factor * below[3] - right_factor * above[3]  5.22 us
    mul x5, other arithmetic, face_terms(): opened * (0.5 * (flux_a + flux_b) - 0.5 * fastest * (state_b - state_a))  4.99 us
    ppermute x2, starting transfers between devices, with_halo(): lax.ppermute(lax.slice_in_dim(block, 0, width, axis=dim), axis, backward)  4.93 us
  transfers between devices with their start and end apart: 5, of which 5 were waited for; matrix products, arithmetic and copies ran while one was open for 4% of the time, Pallas kernels for 0%

profile of v1, /device:TPU:8, one launch (start us, length us, event | category | flops | bytes accessed | tf_op | source)
XLA Modules:
  0.0 113.9 jit_solution(15939293743457586420)
XLA Ops:
  0.7 1.0 bitcast_dynamic-update-slice_fusion.4
  1.7 1.0 bitcast_dynamic-update-slice_fusion.3
  2.7 1.0 bitcast_dynamic-update-slice_fusion.2
  3.7 3.8 %collective-permute-start = (f32[5,2,512]{2,1,0:T(2,128)S(1)}, f32[5,2,512]{2,1,0:T(2,128)S(1)}, u32[]{:S(2)}, u32[]{:S(2)}) collective-permute-start(f32[5,2,512]{2,1,0:T(2,128)S(1)} %get-tuple-element.274), channel_id=1, source_target_pairs={{0,8},{8,16},{16,24},{24,32},{32,40},{40,48},{48,56},{56,64},{64,7... | collective-permute-start | bytes 61448 | tf_op jit(solution)/shard_map/ppermute | solution.py:16
  7.6 1.3 %collective-permute-start.1 = (f32[5,2,512]{2,1,0:T(2,128)S(1)}, f32[5,2,512]{2,1,0:T(2,128)S(1)}, u32[]{:S(2)}, u32[]{:S(2)}) collective-permute-start(f32[5,2,512]{2,1,0:T(2,128)S(1)} %get-tuple-element.275), channel_id=1, source_target_pairs={{8,0},{16,8},{24,16},{32,24},{40,32},{48,40},{56,48},{64,56},{72,6... | collective-permute-start | bytes 61448 | tf_op jit(solution)/shard_map/ppermute | solution.py:19
  9.0 4.2 %collective-permute-done.1 = f32[5,2,512]{2,1,0:T(2,128)S(1)} collective-permute-done((f32[5,2,512]{2,1,0:T(2,128)S(1)}, f32[5,2,512]{2,1,0:T(2,128)S(1)}, u32[]{:S(2)}, u32[]{:S(2)}) %collective-permute-start.1) | collective-permute-done | bytes 20512 | tf_op jit(solution)/shard_map/ppermute | solution.py:19
  13.6 1.9 %collective-permute-start.2 = (f32[5,132,2]{2,1,0:T(8,128)S(1)}, f32[5,132,2]{2,1,0:T(8,128)S(1)}, u32[]{:S(2)}, u32[]{:S(2)}) collective-permute-start(f32[5,132,2]{2,1,0:T(8,128)S(1)} %get-tuple-element.272), channel_id=1, source_target_pairs={{0,1},{1,2},{2,3},{3,4},{4,5},{5,6},{6,7},{8,9},{9,10},{10,11},{11... | collective-permute-start | bytes 15848 | tf_op jit(solution)/shard_map/ppermute | solution.py:16
  15.5 3.6 %collective-permute-start.3 = (f32[5,132,2]{2,1,0:T(8,128)S(1)}, f32[5,132,2]{2,1,0:T(8,128)S(1)}, u32[]{:S(2)}, u32[]{:S(2)}) collective-permute-start(f32[5,132,2]{2,1,0:T(8,128)S(1)} %get-tuple-element.273), channel_id=1, source_target_pairs={{1,0},{2,1},{3,2},{4,3},{5,4},{6,5},{7,6},{9,8},{10,9},{11,10},{12... | collective-permute-start | bytes 15848 | tf_op jit(solution)/shard_map/ppermute | solution.py:19
  20.5 1.1 %fusion.73 = (f32[129,512]{1,0:T(8,128)}, f32[129,512]{1,0:T(8,128)S(1)}) fusion(f32[129,512]{1,0:T(8,128)S(1)} %get-tuple-element.229, f32[129,512]{1,0:T(8,128)S(1)} %get-tuple-element.225, f32[129,512]{1,0:T(8,128)S(1)} %get-tuple-element.226, f32[129,512]{1,0:T(8,128)S(1)} %get-tuple-element.228, f32[129,512]{1,0:T(8,128)S(1)} %get-tuple-element.227), kind=kLoop, calls=%fused_computation.229 | loop fusion | flops 2179584 | bytes 1849344 | tf_op jit(solution)/shard_map/mul | solution.py:66
  22.2 1.8 %collective-permute-done.3 = f32[5,132,2]{2,1,0:T(8,128)S(1)} collective-permute-done((f32[5,132,2]{2,1,0:T(8,128)S(1)}, f32[5,132,2]{2,1,0:T(8,128)S(1)}, u32[]{:S(2)}, u32[]{:S(2)}) %collective-permute-start.3) | collective-permute-done | bytes 5312 | tf_op jit(solution)/shard_map/ppermute | solution.py:19
  25.4 0.8 subtract_multiply_fusion.1
  26.2 0.8 fusion.60
  27.2 1.1 fusion.232
  28.8 1.7 %subtract_multiply_fusion = f32[128,513]{1,0:T(8,128)} fusion(f32[128,514]{1,0:T(8,128)S(1)} %get-tuple-element.331, f32[128,516]{1,0:T(8,128)S(1)} %get-tuple-element.267, f32[128,516]{1,0:T(8,128)S(1)} %maximum_bitcast_fusion.2, f32[128,514]{1,0:T(8,128)S(1)} %minimum_multiply_fusion.2, f32[128,516]{1,0:T(8,128)S(1)} %get-tuple-element.269, ...), kind=kLoop, calls=%fused_computation.213 | loop fusion | flops 2232576 | bytes 3939840 | tf_op jit(solution)/shard_map/mul | solution.py:66
  40.4 6.1 %all-to-all-start = ((f32[8,9,1,128]{3,2,1,0:T(1,128)}), f32[8,9,1,128]{3,2,1,0:T(1,128)S(1)}, u32[]{:S(2)}, u32[]{:S(2)}) async-start(f32[8,9,1,128]{3,2,1,0:T(1,128)} %stack.61), calls=%async_computation | async-start | bytes 73728 | tf_op jit(solution)/shard_map/all_to_all | solution.py:200
  46.5 0.9 negate_multiply_fusion.2
  47.4 0.8 multiply_subtract_fusion.3
  49.0 1.6 %all-to-all-done = f32[8,9,1,128]{3,2,1,0:T(1,128)S(1)} async-done(((f32[8,9,1,128]{3,2,1,0:T(1,128)}), f32[8,9,1,128]{3,2,1,0:T(1,128)S(1)}, u32[]{:S(2)}, u32[]{:S(2)}) %all-to-all-start) | async-done | bytes 36896 | tf_op jit(solution)/shard_map/all_to_all | solution.py:200
  51.0 2.4 %maximum_divide_fusion.1 = (f32[128,512]{1,0:T(8,128)}, f32[128,512]{1,0:T(8,128)S(1)}) fusion(f32[128,512]{1,0:T(8,128)S(1)} %copy-done, f32[128,1]{1,0:T(8,128)S(1)} %copy.35, f32[128,511]{1,0:T(8,128)S(1)} %fusion.224, f32[5,128,512]{2,1,0:T(8,128)S(1)} %bitcast_dynamic-update-slice_fusion, f32[5,2,512]{2,1,0:T(2,128)S(1)} %collective-permute-done, ...), kind=kLoop, calls=%fused_computation.461 | loop fusion | flops 1114112 | bytes 3973120 | tf_op jit(solution)/shard_map/div | solution.py:220
  53.5 0.8 copy-done.3
  54.6 0.7 copy-done.1
  57.9 53.4 %all-gather = f32[9,16384]{1,0:T(8,128)S(1)} all-gather(f32[9,512]{1,0:T(8,128)S(1)} %concatenate.48), channel_id=2, replica_groups=mesh['gx'=32,'gy'=8] {'gx'}, dimensions={1}, use_global_device_ids=true | all-gather | bytes 608256 | tf_op jit(solution)/shard_map/all_gather | solution.py:193
  111.3 1.0 slice_reduce_fusion.4
  113.1 0.8 maximum_divide_fusion
  (147 shorter events, 18.7 us)
Async XLA Ops:
  0.6 3.0 %copy-start.10 = (f32[128,512]{1,0:T(8,128)S(1)}, f32[128,512]{1,0:T(8,128)}, u32[]{:S(2)}) copy-start(f32[128,512]{1,0:T(8,128)} %param.8) | copy-start | bytes 786436
  0.6 3.0 %copy-start.6 = (s32[128,512]{1,0:T(8,128)S(1)}, s32[128,512]{1,0:T(8,128)}, u32[]{:S(2)}) copy-start(s32[128,512]{1,0:T(8,128)} %param.9) | copy-start | bytes 786436
  3.7 5.3 %collective-permute-start = (f32[5,2,512]{2,1,0:T(2,128)S(1)}, f32[5,2,512]{2,1,0:T(2,128)S(1)}, u32[]{:S(2)}, u32[]{:S(2)}) collective-permute-start(f32[5,2,512]{2,1,0:T(2,128)S(1)} %get-tuple-element.274), channel_id=1, source_target_pairs={{0,8},{8,16},{16,24},{24,32},{32,40},{40,48},{48,56},{56,64},{64,7... | collective-permute-start | bytes 61448 | tf_op jit(solution)/shard_map/ppermute | solution.py:16
  7.6 5.7 %collective-permute-start.1 = (f32[5,2,512]{2,1,0:T(2,128)S(1)}, f32[5,2,512]{2,1,0:T(2,128)S(1)}, u32[]{:S(2)}, u32[]{:S(2)}) collective-permute-start(f32[5,2,512]{2,1,0:T(2,128)S(1)} %get-tuple-element.275), channel_id=1, source_target_pairs={{8,0},{16,8},{24,16},{32,24},{40,32},{48,40},{56,48},{64,56},{72,6... | collective-permute-start | bytes 61448 | tf_op jit(solution)/shard_map/ppermute | solution.py:19
  13.6 8.6 %collective-permute-start.2 = (f32[5,132,2]{2,1,0:T(8,128)S(1)}, f32[5,132,2]{2,1,0:T(8,128)S(1)}, u32[]{:S(2)}, u32[]{:S(2)}) collective-permute-start(f32[5,132,2]{2,1,0:T(8,128)S(1)} %get-tuple-element.272), channel_id=1, source_target_pairs={{0,1},{1,2},{2,3},{3,4},{4,5},{5,6},{6,7},{8,9},{9,10},{10,11},{11... | collective-permute-start | bytes 15848 | tf_op jit(solution)/shard_map/ppermute | solution.py:16
  15.5 8.4 %collective-permute-start.3 = (f32[5,132,2]{2,1,0:T(8,128)S(1)}, f32[5,132,2]{2,1,0:T(8,128)S(1)}, u32[]{:S(2)}, u32[]{:S(2)}) collective-permute-start(f32[5,132,2]{2,1,0:T(8,128)S(1)} %get-tuple-element.273), channel_id=1, source_target_pairs={{1,0},{2,1},{3,2},{4,3},{5,4},{6,5},{7,6},{9,8},{10,9},{11,10},{12... | collective-permute-start | bytes 15848 | tf_op jit(solution)/shard_map/ppermute | solution.py:19
  26.2 1.0 copy-start
  26.2 1.0 copy-start.7
  40.4 10.1 %all-to-all-start = ((f32[8,9,1,128]{3,2,1,0:T(1,128)}), f32[8,9,1,128]{3,2,1,0:T(1,128)S(1)}, u32[]{:S(2)}, u32[]{:S(2)}) async-start(f32[8,9,1,128]{3,2,1,0:T(1,128)} %stack.61), calls=%async_computation | async-start | bytes 73728 | tf_op jit(solution)/shard_map/all_to_all | solution.py:200
  47.4 0.9 copy-start.2
  48.3 0.7 copy-start.4
  51.0 2.5 %copy-start.8 = (f32[1,127,512]{2,1,0:T(8,128)S(1)}, f32[1,127,512]{2,1,0:T(8,128)}, u32[]{:S(2)}) copy-start(f32[1,127,512]{2,1,0:T(8,128)} %get-tuple-element.291) | copy-start | bytes 780292
  51.0 2.5 %copy-start.9 = (f32[1,127,512]{2,1,0:T(8,128)S(1)}, f32[1,127,512]{2,1,0:T(8,128)}, u32[]{:S(2)}) copy-start(f32[1,127,512]{2,1,0:T(8,128)} %get-tuple-element.292) | copy-start | bytes 780292
  53.4 0.9 copy-start.3
  53.4 1.0 copy-start.5
  54.4 0.9 copy-start.1
